TPU v7x, 32 devices: a whole 2x2x4 slice. The times are simulated.
32 devices in a mesh: dp: 16 (over z, y, x), head: 2 (over core).
Axes of the slice: x: 2, y: 2, z: 4, core: 2. Of those that a mesh axis runs over, the one named last changes fastest.
Arguments:
- inputs: bfloat16 [16, 2, 512, 768], P('dp'), may hold values from -6 to 6
- cotangent: bfloat16 [16, 2, 512, 768], P('dp'), may hold values from -6 to 6
- seg_counts: int32 [16], P('dp'), may hold values from 1 to 2
- qkv_weight: float32 [3, 768, 768], P(None, 'dp', 'head'), may hold values from -0.3125 to 0.3125
- out_weight: float32 [768, 768], P('head', 'dp'), may hold values from -0.875 to 0.875
- up_weight: float32 [768, 3072], P('dp', 'head'), may hold values from -0.21875 to 0.21875
- down_weight: float32 [3072, 768], P('head', 'dp'), may hold values from -0.109375 to 0.109375
- head_bias: float32 [2, 2304], P('head'), may hold values from -3 to 3
- shared_params: float32 [16, 768], replicated, may hold values from -5 to 5
- qkv_first: float32 [3, 768, 768], P(None, 'dp', 'head'), may hold values from -0.00024414062 to 0.00024414062
- out_first: float32 [768, 768], P('head', 'dp'), may hold values from -0.00024414062 to 0.00024414062
- up_first: float32 [768, 3072], P('dp', 'head'), may hold values from -0.00024414062 to 0.00024414062
- down_first: float32 [3072, 768], P('head', 'dp'), may hold values from -0.00024414062 to 0.00024414062
- bias_first: float32 [2, 2304], P('head'), may hold values from -0.00024414062 to 0.00024414062
- shared_first: float32 [16, 768], replicated, may hold values from -0.00024414062 to 0.00024414062
- qkv_second: float32 [3, 768, 768], P(None, 'dp', 'head'), may hold values from 1.4094861e-10 to 5.6379446e-10
- out_second: float32 [768, 768], P('head', 'dp'), may hold values from 1.4094861e-10 to 5.6379446e-10
- up_second: float32 [768, 3072], P('dp', 'head'), may hold values from 1.4094861e-10 to 5.6379446e-10
- down_second: float32 [3072, 768], P('head', 'dp'), may hold values from 1.4094861e-10 to 5.6379446e-10
- bias_second: float32 [2, 2304], P('head'), may hold values from 1.4094861e-10 to 5.6379446e-10
- shared_second: float32 [16, 768], replicated, may hold values from 1.4094861e-10 to 5.6379446e-10
Outputs:
- outputs: bfloat16 [16, 2, 512, 768], P('dp')
- input_grad: bfloat16 [16, 2, 512, 768], P('dp')
- grad_norm: float32 [], replicated
- qkv_update: float32 [3, 768, 768], P(None, 'dp', 'head')
- out_update: float32 [768, 768], P('head', 'dp')
- up_update: float32 [768, 3072], P('dp', 'head')
- down_update: float32 [3072, 768], P('head', 'dp')
- bias_update: float32 [2, 2304], P('head')
- shared_update: float32 [16, 768], replicated
- qkv_moment: float32 [3, 768, 768], P(None, 'dp', 'head')
- out_moment: float32 [768, 768], P('head', 'dp')
- up_moment: float32 [768, 3072], P('dp', 'head')
- down_moment: float32 [3072, 768], P('head', 'dp')
- bias_moment: float32 [2, 2304], P('head')
- shared_moment: float32 [16, 768], replicated
- qkv_square: float32 [3, 768, 768], P(None, 'dp', 'head')
- out_square: float32 [768, 768], P('head', 'dp')
- up_square: float32 [768, 3072], P('dp', 'head')
- down_square: float32 [3072, 768], P('head', 'dp')
- bias_square: float32 [2, 2304], P('head')
- shared_square: float32 [16, 768], replicated
Inputs may be any that keep to these rules, and one draw needn't show every extreme that they name: `seg_counts`: a chain's slots 0 to its count minus 1 are live.
All inputs are finite; a program needn't handle non-finite values.
Results may differ from a plain program's by a relative error of at most 0.02.
The roundings to bfloat16 on the way count: a program that leaves them out, or rounds other values in their place, can miss the bound.
Values may be sent and summed in bfloat16 or wider, within the bound.
No kernel may reach another device: no remote copies, remote signals or barrier semaphores. Data moves between devices by JAX's collectives and lax.ppermute only.
A program may use at most 192 MiB of HBM per device.

v0:
```python
import jax
import jax.numpy as jnp
from jax import lax
from jax.sharding import PartitionSpec as P

HD = 64
STEP = 10
EPSILON = 1e-06
BETA_ONE = 0.9
BETA_TWO = 0.999
LEARN_RATE = 0.1
VECTOR_RATE = 0.6
DECAY_RATE = 0.01
ADAM_EPSILON = 1e-08
CLIP_NORM = 1.0


def norm_rows(values, gain, shift):
    average = jnp.mean(values, axis=-1, keepdims=True)
    centered = values - average
    variance = jnp.mean(centered * centered, axis=-1, keepdims=True)
    return centered * lax.rsqrt(variance + EPSILON) * gain + shift


def gelu_exact(values):
    return jax.nn.gelu(values, approximate=False)


def adam_update(weight, first_old, second_old, gradient, factor, decay_rate, step_rate):
    clipped = gradient * factor
    first_new = BETA_ONE * first_old + (1.0 - BETA_ONE) * clipped
    second_new = BETA_TWO * second_old + (1.0 - BETA_TWO) * clipped * clipped
    first_hat = first_new / (1.0 - BETA_ONE**STEP)
    second_hat = second_new / (1.0 - BETA_TWO**STEP)
    weight_new = weight - step_rate * (
        first_hat / (jnp.sqrt(second_hat) + ADAM_EPSILON) + decay_rate * weight
    )
    return (weight_new, first_new, second_new)


def square_sum(arrays):
    return sum((jnp.sum(member * member) for member in arrays))


def shards(
    inputs,
    cotangent,
    seg_counts,
    qkv_weight,
    out_weight,
    up_weight,
    down_weight,
    head_bias,
    shared_params,
    qkv_first,
    out_first,
    up_first,
    down_first,
    bias_first,
    shared_first,
    qkv_second,
    out_second,
    up_second,
    down_second,
    bias_second,
    shared_second,
):
    chains, segments, seg_len, model_width = inputs.shape
    mem_count = shared_params.shape[0] - 6
    seg_rows = seg_len + 2 * mem_count
    local_width = qkv_weight.shape[2]
    head_local = local_width // HD
    score_scale = HD ** (-0.5)
    bfloat = jnp.bfloat16
    single = jnp.float32
    qkv_full, out_full, up_full, down_full = (
        lax.all_gather(qkv_weight.astype(bfloat), "dp", axis=1, tiled=True),
        lax.all_gather(out_weight.astype(bfloat), "dp", axis=1, tiled=True),
        lax.all_gather(up_weight.astype(bfloat), "dp", axis=0, tiled=True),
        lax.all_gather(down_weight.astype(bfloat), "dp", axis=1, tiled=True),
    )
    q_bias = head_bias[0, :local_width]
    v_bias = head_bias[0, local_width : 2 * local_width]
    up_bias = head_bias[0, 2 * local_width :]
    out_bias = shared_params[mem_count]
    down_bias = shared_params[mem_count + 1]
    gain_one = shared_params[mem_count + 2]
    shift_one = shared_params[mem_count + 3]
    gain_two = shared_params[mem_count + 4]
    shift_two = shared_params[mem_count + 5]
    alive_all = (jnp.arange(segments, dtype=jnp.int32)[None, :] < seg_counts[:, None]).astype(
        single
    )
    memory = shared_params[:mem_count][None]
    stored = []
    token_list = []
    for segment in range(segments):
        alive_mask = alive_all[:, segment][:, None, None]
        layer_in = jnp.concatenate([memory, inputs[:, segment].astype(single), memory], axis=1)
        layer_low = layer_in.astype(bfloat)
        projected = jnp.einsum("cld,tde->tcle", layer_low, qkv_full, preferred_element_type=single)
        query_low = (projected[0] + q_bias).astype(bfloat).reshape(chains, seg_rows, head_local, HD)
        key_low = projected[1].astype(bfloat).reshape(chains, seg_rows, head_local, HD)
        value_low = (projected[2] + v_bias).astype(bfloat).reshape(chains, seg_rows, head_local, HD)
        scores = (
            jnp.einsum("cqhe,ckhe->chqk", query_low, key_low, preferred_element_type=single)
            * score_scale
        )
        log_total = jax.nn.logsumexp(scores, axis=-1, keepdims=True)
        chance_low = jnp.exp(scores - log_total).astype(bfloat)
        context_low = (
            jnp.einsum("chqk,ckhe->cqhe", chance_low, value_low, preferred_element_type=single)
            .reshape(chains, seg_rows, local_width)
            .astype(bfloat)
        )
        attn_part = jnp.einsum("cle,ed->cld", context_low, out_full, preferred_element_type=single)
        attn_out = lax.psum(attn_part.astype(jnp.bfloat16), "head").astype(jnp.float32)
        first_in = layer_in + attn_out + out_bias
        hidden = norm_rows(first_in, gain_one, shift_one)
        hidden_low = hidden.astype(bfloat)
        upper_in = (
            jnp.einsum("cld,de->cle", hidden_low, up_full, preferred_element_type=single) + up_bias
        )
        active_low = gelu_exact(upper_in).astype(bfloat)
        ffn_part = jnp.einsum("cle,ed->cld", active_low, down_full, preferred_element_type=single)
        ffn_out = lax.psum(ffn_part.astype(jnp.bfloat16), "head").astype(jnp.float32)
        second_in = hidden + ffn_out + down_bias
        result = norm_rows(second_in, gain_two, shift_two)
        token_list.append(result[:, mem_count : mem_count + seg_len] * alive_mask)
        memory = jnp.where(alive_mask > 0, result[:, mem_count + seg_len :], memory)
        stored.append(
            (
                layer_in,
                query_low,
                key_low,
                value_low,
                log_total,
                context_low,
                first_in,
                hidden,
                upper_in,
                active_low,
                second_in,
            )
        )
    outputs = jnp.stack(token_list, axis=1).astype(bfloat)
    grad_qkv = jnp.zeros(qkv_full.shape, single)
    grad_out = jnp.zeros(out_full.shape, single)
    grad_up = jnp.zeros(up_full.shape, single)
    grad_down = jnp.zeros(down_full.shape, single)
    grad_qbias = jnp.zeros((local_width,), single)
    grad_vbias = jnp.zeros((local_width,), single)
    grad_upbias = jnp.zeros(up_bias.shape, single)
    vector_grads = jnp.zeros((6, model_width), single)
    memory_grad = jnp.zeros((chains, mem_count, model_width), single)
    grad_list = [None] * segments
    for segment in reversed(range(segments)):
        (
            layer_in,
            query_low,
            key_low,
            value_low,
            log_total,
            context_low,
            first_in,
            hidden,
            upper_in,
            active_low,
            second_in,
        ) = stored[segment]
        alive_mask = alive_all[:, segment][:, None, None]
        result_grad = jnp.concatenate(
            [
                jnp.zeros((chains, mem_count, model_width), single),
                cotangent[:, segment].astype(single) * alive_mask,
                memory_grad * alive_mask,
            ],
            axis=1,
        )
        unused, norm_two_back = jax.vjp(norm_rows, second_in, gain_two, shift_two)
        second_grad, gain_two_grad, shift_two_grad = norm_two_back(result_grad)
        ffn_grad_low = second_grad.astype(bfloat)
        grad_down = grad_down + jnp.einsum(
            "cle,cld->ed", active_low, ffn_grad_low, preferred_element_type=single
        )
        active_grad = jnp.einsum(
            "cld,ed->cle", ffn_grad_low, down_full, preferred_element_type=single
        )
        unused, gelu_back = jax.vjp(gelu_exact, upper_in)
        (upper_grad,) = gelu_back(active_grad)
        grad_upbias = grad_upbias + jnp.sum(upper_grad, axis=(0, 1))
        upper_low = upper_grad.astype(bfloat)
        hidden_low = hidden.astype(bfloat)
        grad_up = grad_up + jnp.einsum(
            "cld,cle->de", hidden_low, upper_low, preferred_element_type=single
        )
        hidden_part = jnp.einsum("cle,de->cld", upper_low, up_full, preferred_element_type=single)
        hidden_grad = second_grad + lax.psum(hidden_part.astype(jnp.bfloat16), "head").astype(
            jnp.float32
        )
        unused, norm_one_back = jax.vjp(norm_rows, first_in, gain_one, shift_one)
        first_grad, gain_one_grad, shift_one_grad = norm_one_back(hidden_grad)
        attn_low = first_grad.astype(bfloat)
        grad_out = grad_out + jnp.einsum(
            "cle,cld->ed", context_low, attn_low, preferred_element_type=single
        )
        context_grad = jnp.einsum("cld,ed->cle", attn_low, out_full, preferred_element_type=single)
        context_grad = context_grad.astype(bfloat).reshape(chains, seg_rows, head_local, HD)
        chance_grad = jnp.einsum(
            "cqhe,ckhe->chqk", context_grad, value_low, preferred_element_type=single
        )
        scores = (
            jnp.einsum("cqhe,ckhe->chqk", query_low, key_low, preferred_element_type=single)
            * score_scale
        )
        chances = jnp.exp(scores - log_total)
        value_grad = jnp.einsum(
            "chqk,cqhe->ckhe", chances.astype(bfloat), context_grad, preferred_element_type=single
        )
        weighted = jnp.sum(chances * chance_grad, axis=-1, keepdims=True)
        score_low = (chances * (chance_grad - weighted)).astype(bfloat)
        query_grad = (
            jnp.einsum("chqk,ckhe->cqhe", score_low, key_low, preferred_element_type=single)
            * score_scale
        )
        key_grad = (
            jnp.einsum("chqk,cqhe->ckhe", score_low, query_low, preferred_element_type=single)
            * score_scale
        )
        query_grad = query_grad.reshape(chains, seg_rows, local_width)
        key_grad = key_grad.reshape(chains, seg_rows, local_width)
        value_grad = value_grad.reshape(chains, seg_rows, local_width)
        grad_qbias = grad_qbias + jnp.sum(query_grad, axis=(0, 1))
        grad_vbias = grad_vbias + jnp.sum(value_grad, axis=(0, 1))
        project_low = jnp.stack([query_grad, key_grad, value_grad]).astype(bfloat)
        grad_qkv = grad_qkv + jnp.einsum(
            "cld,tcle->tde", layer_in.astype(bfloat), project_low, preferred_element_type=single
        )
        rows_part = jnp.einsum(
            "tcle,tde->cld", project_low, qkv_full, preferred_element_type=single
        )
        rows_grad = first_grad + lax.psum(rows_part.astype(jnp.bfloat16), "head").astype(
            jnp.float32
        )
        grad_list[segment] = rows_grad[:, mem_count : mem_count + seg_len] * alive_mask
        memory_new = rows_grad[:, :mem_count] + rows_grad[:, mem_count + seg_len :]
        memory_grad = jnp.where(alive_mask > 0, memory_new, memory_grad)
        vector_grads = vector_grads + jnp.stack(
            [
                jnp.sum(first_grad, axis=(0, 1)),
                jnp.sum(second_grad, axis=(0, 1)),
                gain_one_grad,
                shift_one_grad,
                gain_two_grad,
                shift_two_grad,
            ]
        )
    input_grad = jnp.stack(grad_list, axis=1).astype(bfloat)
    head_grad = jnp.concatenate([grad_qbias, grad_vbias, grad_upbias])[None]
    shared_grad = jnp.concatenate([jnp.sum(memory_grad, axis=0), vector_grads], axis=0)
    dp_index = lax.axis_index("dp")
    summed = lax.psum((grad_qkv, grad_out, grad_up, grad_down, head_grad, shared_grad), "dp")
    head_squares = square_sum(summed[:5])
    squares_total = lax.psum(head_squares, "head") + square_sum((summed[5],))
    qkv_block = qkv_weight.shape[1]
    out_block = out_weight.shape[1]
    up_block = up_weight.shape[0]
    down_block = down_weight.shape[1]
    qkv_grad = lax.dynamic_slice_in_dim(summed[0], dp_index * qkv_block, qkv_block, 1)
    out_grad = lax.dynamic_slice_in_dim(summed[1], dp_index * out_block, out_block, 1)
    up_grad = lax.dynamic_slice_in_dim(summed[2], dp_index * up_block, up_block, 0)
    down_grad = lax.dynamic_slice_in_dim(summed[3], dp_index * down_block, down_block, 1)
    bias_grad = summed[4]
    common_grad = summed[5]
    grad_norm = jnp.sqrt(squares_total)
    factor = CLIP_NORM / jnp.maximum(grad_norm, CLIP_NORM)
    qkv_result = adam_update(
        qkv_weight, qkv_first, qkv_second, qkv_grad, factor, DECAY_RATE, LEARN_RATE
    )
    out_result = adam_update(
        out_weight, out_first, out_second, out_grad, factor, DECAY_RATE, LEARN_RATE
    )
    up_result = adam_update(up_weight, up_first, up_second, up_grad, factor, DECAY_RATE, LEARN_RATE)
    down_result = adam_update(
        down_weight, down_first, down_second, down_grad, factor, DECAY_RATE, LEARN_RATE
    )
    bias_result = adam_update(
        head_bias, bias_first, bias_second, bias_grad, factor, 0.0, VECTOR_RATE
    )
    shared_result = adam_update(
        shared_params, shared_first, shared_second, common_grad, factor, 0.0, VECTOR_RATE
    )
    return (
        outputs,
        input_grad,
        grad_norm,
        qkv_result[0],
        out_result[0],
        up_result[0],
        down_result[0],
        bias_result[0],
        shared_result[0],
        qkv_result[1],
        out_result[1],
        up_result[1],
        down_result[1],
        bias_result[1],
        shared_result[1],
        qkv_result[2],
        out_result[2],
        up_result[2],
        down_result[2],
        bias_result[2],
        shared_result[2],
    )


def solution(mesh):
    return jax.shard_map(
        shards,
        mesh=mesh,
        in_specs=(
            P("dp", None, None, None),
            P("dp", None, None, None),
            P("dp"),
            P(None, "dp", "head"),
            P("head", "dp"),
            P("dp", "head"),
            P("head", "dp"),
            P("head", None),
            P(),
            P(None, "dp", "head"),
            P("head", "dp"),
            P("dp", "head"),
            P("head", "dp"),
            P("head", None),
            P(),
            P(None, "dp", "head"),
            P("head", "dp"),
            P("dp", "head"),
            P("head", "dp"),
            P("head", None),
            P(),
        ),
        out_specs=(
            P("dp", None, None, None),
            P("dp", None, None, None),
            P(),
            P(None, "dp", "head"),
            P("head", "dp"),
            P("dp", "head"),
            P("head", "dp"),
            P("head", None),
            P(),
            P(None, "dp", "head"),
            P("head", "dp"),
            P("dp", "head"),
            P("head", "dp"),
            P("head", None),
            P(),
            P(None, "dp", "head"),
            P("head", "dp"),
            P("dp", "head"),
            P("head", "dp"),
            P("head", None),
            P(),
        ),
        check_vma=False,
    )
```

profile of v0, /device:TPU:0, one launch (start us, length us, event | category | flops | bytes accessed | tf_op | source)
XLA Modules:
  0.0 962.0 jit_solution(8777795133562710844)
XLA Ops:
  11.5 47.0 %all_gather.13 = bf16[384,768]{0,1:T(8,128)(2,1)S(1)} all-gather(bf16[384,48]{0,1:T(8,128)(2,1)S(1)} %convert_element_type.373), channel_id=1, replica_groups=mesh['dp'=16,'head'=2] {'dp'}, dimensions={1}, use_global_device_ids=true | all-gather | bytes 626688 | tf_op jit(solution)/shard_map/all_gather | solution.py:78
  58.5 3.4 bitcast_convert_fusion.2
  61.8 12.4 %all-gather.4.cloned.1.call-done = bf16[3,768,384]{2,1,0:T(8,128)(2,1)} async-done(((bf16[3,48,384]{2,1,0:T(8,128)(2,1)}), bf16[3,768,384]{2,1,0:T(8,128)(2,1)}) %all-gather.4.cloned.1.call-update) | async-done | bytes 1769488 | tf_op jit(solution)/shard_map/all_gather | solution.py:77
  74.2 2.7 convolution_bitcast_fusion.1
  80.8 2.9 multiply_reduce_fusion.3
  88.4 5.3 convolution_convert_fusion.7
  98.0 16.3 %all-reduce.12.cloned.1.call-done = bf16[1,532,768]{2,1,0:T(8,128)(2,1)} async-done(((bf16[1,532,768]{2,1,0:T(8,128)(2,1)}), bf16[1,532,768]{2,1,0:T(8,128)(2,1)}) %all-reduce.12.cloned.1.call-update) | async-done | bytes 817168 | tf_op jit(solution)/shard_map/psum | solution.py:117
  116.2 65.4 %all-gather.6.cloned.1.call-done = bf16[768,1536]{1,0:T(8,128)(2,1)} async-done(((bf16[48,1536]{1,0:T(8,128)(2,1)}), bf16[768,1536]{1,0:T(8,128)(2,1)}) %all-gather.6.cloned.1.call-update) | async-done | bytes 2359312 | tf_op jit(solution)/shard_map/all_gather | solution.py:79
  181.6 11.6 %multiply_convert_fusion.3 = (bf16[532,1536]{1,0:T(8,128)(2,1)S(1)}, f32[532,1536]{1,0:T(8,128)}, f32[532,1536]{1,0:T(8,128)}) fusion(f32[1536]{0:T(1024)S(1)} %slice_reduce_fusion, bf16[768,1536]{1,0:T(8,128)(2,1)} %all-gather.6.cloned.1.call-done, f32[1,532,768]{2,1,0:T(8,128)S(1)} %get-tuple-element.134, f32[768]{0:T(1024)S(1)} %get-tuple-element.80, ...), kind=kOutput, calls=%fused_computation.37 | convolution fusion | flops 1311120384 | bytes 12181664 | tf_op jit(solution)/shard_map/cld,de->cle/dot_general | solution.py:122
  193.1 53.2 %all-gather.8.cloned.1.call-done = bf16[1536,768]{0,1:T(8,128)(2,1)} async-done(((bf16[1536,48]{0,1:T(8,128)(2,1)}), bf16[1536,768]{0,1:T(8,128)(2,1)}) %all-gather.8.cloned.1.call-update) | async-done | bytes 2359312 | tf_op jit(solution)/shard_map/all_gather | solution.py:80
  246.3 4.0 fusion.32
  252.3 16.3 %all-reduce.14.cloned.1.call-done = bf16[1,532,768]{2,1,0:T(8,128)(2,1)} async-done(((bf16[1,532,768]{2,1,0:T(8,128)(2,1)}), bf16[1,532,768]{2,1,0:T(8,128)(2,1)}) %all-reduce.14.cloned.1.call-update) | async-done | bytes 817168 | tf_op jit(solution)/shard_map/psum | solution.py:126
  282.7 5.3 convolution_convert_fusion.6
  290.7 20.4 %all-reduce.16.cloned.1.call-done = bf16[1,532,768]{2,1,0:T(8,128)(2,1)} async-done(((bf16[1,532,768]{2,1,0:T(8,128)(2,1)}), bf16[1,532,768]{2,1,0:T(8,128)(2,1)}) %all-reduce.16.cloned.1.call-update) | async-done | bytes 817168 | tf_op jit(solution)/shard_map/psum | solution.py:117
  311.0 2.2 fusion.124
  314.0 10.0 %multiply_convert_fusion.2 = (bf16[532,1536]{1,0:T(8,128)(2,1)S(1)}, f32[532,1536]{1,0:T(8,128)}, f32[532,1536]{1,0:T(8,128)}) fusion(f32[1536]{0:T(1024)S(1)} %copy-done.101, bf16[768,1536]{1,0:T(8,128)(2,1)S(1)} %copy-done.102, f32[1,532,768]{2,1,0:T(8,128)S(1)} %get-tuple-element.126, f32[532]{0:T(1024)S(1)} %fusion.77, ...), kind=kOutput, calls=%fused_computation.24 | convolution fusion | flops 1311120384 | bytes 12181664 | tf_op jit(solution)/shard_map/cld,de->cle/dot_general | solution.py:122
  325.2 2.4 fusion.33
  328.4 4.6 fusion.26
  333.0 15.2 %all-reduce.18.cloned.1.call-done = bf16[1,532,768]{2,1,0:T(8,128)(2,1)} async-done(((bf16[1,532,768]{2,1,0:T(8,128)(2,1)}), bf16[1,532,768]{2,1,0:T(8,128)(2,1)}) %all-reduce.18.cloned.1.call-update) | async-done | bytes 817168 | tf_op jit(solution)/shard_map/psum | solution.py:126
  348.2 2.0 fusion.122
  354.1 2.5 fusion.137
  357.8 2.4 fusion.34
  361.4 19.5 %all-reduce.20.cloned.1.call-done = bf16[1,532,768]{2,1,0:T(8,128)(2,1)} async-done(((bf16[1,532,768]{2,1,0:T(8,128)(2,1)}), bf16[1,532,768]{2,1,0:T(8,128)(2,1)}) %all-reduce.20.cloned.1.call-update) | async-done | bytes 817168 | tf_op jit(solution)/shard_map/psum | solution.py:198
  380.9 2.8 multiply_reduce_fusion.10
  387.4 2.0 copy.140
  389.4 6.0 fusion.135
  395.4 4.7 multiply_reduce_fusion.1
  400.2 2.1 multiply_convert_fusion.1
  402.3 2.2 fusion.40
  406.3 2.0 copy.146
  408.2 2.0 copy.145
  410.2 2.0 copy.144
  412.2 4.1 fusion.38
  416.5 6.3 fusion.99
  422.9 4.3 fusion.50
  427.2 1.9 fusion.96
  429.1 7.8 all-reduce.22.cloned.1.call-done
  436.9 2.0 add_reduce_fusion.2
  440.2 4.5 multiply_reduce_fusion.7
  446.4 2.7 fusion.138
  450.3 2.4 fusion.35
  453.0 4.6 fusion.61
  457.6 6.9 convolution_add_fusion.1
  464.5 8.8 all-reduce.24.cloned.1.call-done
  473.3 2.2 multiply_reduce_fusion.8
  478.7 5.1 fusion.134
  483.8 4.9 multiply_reduce_fusion
  488.8 2.1 multiply_convert_fusion
  495.6 3.9 fusion.39
  499.6 7.3 convolution_add_fusion
  507.0 1.9 convolution_add_fusion.4
  508.9 3.7 add_bitcast_fusion
  514.0 3.7 fusion.54
  518.0 2.2 all-reduce.26.cloned.1.call-done
  520.2 2.6 add_reduce_fusion
  523.7 81.7 %all-reduce = (f32[1,2304]{1,0:T(1,128)S(1)}, f32[16,768]{1,0:T(8,128)S(1)}) all-reduce(f32[1,2304]{1,0:T(1,128)S(1)} %broadcast_in_dim.95, f32[16,768]{1,0:T(8,128)S(1)} %pad_maximum_fusion.10), channel_id=1, replica_groups=mesh['dp'=16,'head'=2] {'dp'}, use_global_device_ids=true, to_apply=%region_44.45 | all-reduce | flops 14592 | bytes 116736 | tf_op jit(solution)/shard_map/psum | solution.py:262
  606.1 3.0 fusion.53
  611.9 314.1 %all-reduce.28.cloned.1.call-done = (f32[3,768,384]{2,1,0:T(8,128)}, f32[384,768]{0,1:T(8,128)}, f32[768,1536]{1,0:T(8,128)}, f32[1536,768]{0,1:T(8,128)}) async-done(((f32[3,768,384]{2,1,0:T(8,128)}, f32[384,768]{0,1:T(8,128)}, f32[768,1536]{1,0:T(8,128)}, f32[1536,768]{0,1:T(8,128)}), (f32[3,768,384]{2,1,0:T(8,128)}, f32[384,768]{0,1:T(8,128)}, f32[768,1536]{1,0:T(8,128)}, ...) | async-done | bytes 14155792 | tf_op jit(solution)/shard_map/psum | solution.py:262
  926.0 3.7 multiply_reduce_fusion.6
  929.7 2.2 multiply_reduce_fusion.19
  940.0 3.0 psum.118
  944.3 1.9 multiply_subtract_fusion.2
  948.0 2.1 multiply_subtract_fusion.1
  950.1 2.0 multiply_subtract_fusion
  (380 shorter events, 75.0 us)
Async XLA Ops:
  7.2 67.0 %all-gather.4.cloned.1.call-start = ((), (), s32[]{:S(2)}) async-start(), calls=%async_computation | async-start | bytes 1880064 | tf_op jit(solution)/shard_map/all_gather | solution.py:77
  8.9 105.4 %all-reduce.12.cloned.1.call-start = ((), (), s32[]{:S(2)}) async-start(), calls=%async_computation.1 | async-start | bytes 1646592 | tf_op jit(solution)/shard_map/psum | solution.py:117
  9.7 64.5 %copy-start.94 = (bf16[10,768]{1,0:T(8,128)(2,1)}, bf16[10,768]{1,0:T(8,128)(2,1)S(1)}, u32[]{:S(2)}) copy-start(bf16[10,768]{1,0:T(8,128)(2,1)S(1)} %slice.211) | copy-start | bytes 46084
  58.5 35.2 %copy-start.29 = (bf16[384,768]{0,1:T(8,128)(2,1)}, bf16[384,768]{0,1:T(8,128)(2,1)S(1)}, u32[]{:S(2)}) copy-start(bf16[384,768]{0,1:T(8,128)(2,1)S(1)} %all_gather.13) | copy-start | bytes 1769476
  61.8 12.4 %copy-start.53 = (bf16[512,768]{1,0:T(8,128)(2,1)}, bf16[512,768]{1,0:T(8,128)(2,1)S(1)}, u32[]{:S(2)}) copy-start(bf16[512,768]{1,0:T(8,128)(2,1)S(1)} %get-tuple-element.146) | copy-start | bytes 2359300
  86.9 6.8 copy-start.60
  88.4 5.3 copy-start.20
  96.1 85.5 %all-gather.6.cloned.1.call-start = ((), (), s32[]{:S(2)}) async-start(), calls=%async_computation.2 | async-start | bytes 2506752 | tf_op jit(solution)/shard_map/all_gather | solution.py:79
  96.8 149.5 %all-gather.8.cloned.1.call-start = ((), (), s32[]{:S(2)}) async-start(), calls=%async_computation.3 | async-start | bytes 2506752 | tf_op jit(solution)/shard_map/all_gather | solution.py:80
  97.6 171.0 %all-reduce.14.cloned.1.call-start = ((), (), s32[]{:S(2)}) async-start(), calls=%async_computation.4 | async-start | bytes 1646592 | tf_op jit(solution)/shard_map/psum | solution.py:126
  97.9 83.7 %copy-start.100 = (f32[1536]{0:T(1024)}, f32[1536]{0:T(1024)S(1)}, u32[]{:S(2)}) copy-start(f32[1536]{0:T(1024)S(1)} %slice_reduce_fusion) | copy-start | bytes 18436
  97.9 17.9 %copy-start.86 = (f32[768]{0:T(1024)}, f32[768]{0:T(1024)S(1)}, u32[]{:S(2)}) copy-start(f32[768]{0:T(1024)S(1)} %get-tuple-element.82) | copy-start | bytes 9220
  97.9 170.7 %copy-start.82 = (f32[768]{0:T(1024)}, f32[768]{0:T(1024)S(1)}, u32[]{:S(2)}) copy-start(f32[768]{0:T(1024)S(1)} %get-tuple-element.80) | copy-start | bytes 9220
  98.0 170.7 %copy-start.84 = (f32[768]{0:T(1024)}, f32[768]{0:T(1024)S(1)}, u32[]{:S(2)}) copy-start(f32[768]{0:T(1024)S(1)} %get-tuple-element.79) | copy-start | bytes 9220
  98.0 172.8 %copy-start.80 = (f32[768]{0:T(1024)}, f32[768]{0:T(1024)S(1)}, u32[]{:S(2)}) copy-start(f32[768]{0:T(1024)S(1)} %get-tuple-element.83) | copy-start | bytes 9220
  116.2 76.9 %copy-start.88 = (f32[532]{0:T(1024)}, f32[532]{0:T(1024)S(1)}, u32[]{:S(2)}) copy-start(f32[532]{0:T(1024)S(1)} %multiply_reduce_fusion.18) | copy-start | bytes 6388
  193.1 57.2 %copy-start.34 = (bf16[532,1536]{1,0:T(8,128)(2,1)}, bf16[532,1536]{1,0:T(8,128)(2,1)S(1)}, u32[]{:S(2)}) copy-start(bf16[532,1536]{1,0:T(8,128)(2,1)S(1)} %get-tuple-element.131) | copy-start | bytes 4902916
  250.4 60.6 %all-reduce.16.cloned.1.call-start = ((), (), s32[]{:S(2)}) async-start(), calls=%async_computation.5 | async-start | bytes 1646592 | tf_op jit(solution)/shard_map/psum | solution.py:117
  282.7 5.4 copy-start.22
  282.7 6.1 copy-start.30
  288.1 22.9 %copy-start.87 = (f32[768]{0:T(1024)S(1)}, f32[768]{0:T(1024)}, u32[]{:S(2)}) copy-start(f32[768]{0:T(1024)} %copy-done.86) | copy-start | bytes 9220
  290.4 57.9 %all-reduce.18.cloned.1.call-start = ((), (), s32[]{:S(2)}) async-start(), calls=%async_computation.6 | async-start | bytes 1646592 | tf_op jit(solution)/shard_map/psum | solution.py:126
  314.0 11.2 %copy-start.105 = (bf16[1536,768]{0,1:T(8,128)(2,1)S(1)}, bf16[1536,768]{0,1:T(8,128)(2,1)}, u32[]{:S(2)}) copy-start(bf16[1536,768]{0,1:T(8,128)(2,1)} %all-gather.8.cloned.1.call-done) | copy-start | bytes 7077892
  327.6 53.3 %all-reduce.20.cloned.1.call-start = ((), (), s32[]{:S(2)}) async-start(), calls=%async_computation.7 | async-start | bytes 1646592 | tf_op jit(solution)/shard_map/psum | solution.py:198
  328.4 19.9 %copy-start.85 = (f32[768]{0:T(1024)S(1)}, f32[768]{0:T(1024)}, u32[]{:S(2)}) copy-start(f32[768]{0:T(1024)} %copy-done.84) | copy-start | bytes 9220
  352.2 4.4 copy-start.11
  360.3 76.7 %all-reduce.22.cloned.1.call-start = ((), (), s32[]{:S(2)}) async-start(), calls=%async_computation.8 | async-start | bytes 1646592 | tf_op jit(solution)/shard_map/psum | solution.py:242
  389.4 6.0 copy-start.23
  389.4 6.0 copy-start.40
  389.4 10.8 %slice-start.2 = ((s8[8232960]{0:T(1024)(128)(4,1)}), s8[4194304]{0:T(1024)(128)(4,1)S(1)}, s32[]{:S(2)}) async-start(s8[8232960]{0:T(1024)(128)(4,1)} %bitcast.210), calls=%async_computation.14 | async-start | bytes 8388608
  395.4 4.7 slice-start.3
  416.3 57.0 %all-reduce.24.cloned.1.call-start = ((), (), s32[]{:S(2)}) async-start(), calls=%async_computation.9 | async-start | bytes 1646592 | tf_op jit(solution)/shard_map/psum | solution.py:198
  416.5 6.3 copy-start.114
  422.9 4.3 copy-start.36
  429.1 11.1 %copy-start.3 = (f32[1,532,768]{2,1,0:T(8,128)S(1)}, f32[1,532,768]{2,1,0:T(8,128)}, u32[]{:S(2)}) copy-start(f32[1,532,768]{2,1,0:T(8,128)} %copy-done.2) | copy-start | bytes 4902916
  440.2 4.5 copy-start.91
  440.2 4.5 copy-start.15
  440.2 5.3 copy-start.115
  440.2 5.3 copy-start.116
  452.7 67.5 %all-reduce.26.cloned.1.call-start = ((), (), s32[]{:S(2)}) async-start(), calls=%async_computation.10 | async-start | bytes 1646592 | tf_op jit(solution)/shard_map/psum | solution.py:242
  453.0 4.6 copy-start.111
  457.6 15.7 %copy-start.5 = (f32[1,532,768]{2,1,0:T(8,128)S(1)}, f32[1,532,768]{2,1,0:T(8,128)}, u32[]{:S(2)}) copy-start(f32[1,532,768]{2,1,0:T(8,128)} %copy-done.4) | copy-start | bytes 4902916
  464.5 11.0 %copy-start.89 = (f32[532]{0:T(1024)S(1)}, f32[532]{0:T(1024)}, u32[]{:S(2)}) copy-start(f32[532]{0:T(1024)} %copy-done.88) | copy-start | bytes 6388
  478.7 5.2 copy-start.21
  478.7 10.1 %slice-start = ((s8[8232960]{0:T(1024)(128)(4,1)}), s8[4194304]{0:T(1024)(128)(4,1)S(1)}, s32[]{:S(2)}) async-start(s8[8232960]{0:T(1024)(128)(4,1)} %bitcast.208), calls=%async_computation.12 | async-start | bytes 8388608
  483.8 5.0 slice-start.1
  499.6 7.4 copy-start.10
  499.6 426.5 %all-reduce.28.cloned.1.call-start = ((), (), s32[]{:S(2)}) async-start(), calls=%async_computation.11 | async-start | bytes 28311552 | tf_op jit(solution)/shard_map/psum | solution.py:262
  499.6 7.3 copy-start.33
  499.6 7.3 copy-start.42
  499.6 9.2 copy-start.109
  926.0 5.8 copy-start.28
  934.2 10.1 %copy-start.52 = (f32[3,48,384]{2,1,0:T(8,128)S(1)}, f32[3,48,384]{2,1,0:T(8,128)}, u32[]{:S(2)}) copy-start(f32[3,48,384]{2,1,0:T(8,128)} %param.24) | copy-start | bytes 663556
  934.2 10.1 %copy-start.74 = (f32[3,48,384]{2,1,0:T(8,128)S(1)}, f32[3,48,384]{2,1,0:T(8,128)}, u32[]{:S(2)}) copy-start(f32[3,48,384]{2,1,0:T(8,128)} %param.30) | copy-start | bytes 663556
  934.2 10.1 %copy-start.75 = (f32[3,48,384]{2,1,0:T(8,128)S(1)}, f32[3,48,384]{2,1,0:T(8,128)}, u32[]{:S(2)}) copy-start(f32[3,48,384]{2,1,0:T(8,128)} %param.36) | copy-start | bytes 663556
  936.0 10.2 %copy-start.73 = (f32[384,48]{0,1:T(8,128)S(1)}, f32[384,48]{0,1:T(8,128)}, u32[]{:S(2)}) copy-start(f32[384,48]{0,1:T(8,128)} %param.25) | copy-start | bytes 221188
  936.0 10.2 %copy-start.76 = (f32[384,48]{0,1:T(8,128)S(1)}, f32[384,48]{0,1:T(8,128)}, u32[]{:S(2)}) copy-start(f32[384,48]{0,1:T(8,128)} %param.31) | copy-start | bytes 221188
  936.0 10.2 %copy-start.77 = (f32[384,48]{0,1:T(8,128)S(1)}, f32[384,48]{0,1:T(8,128)}, u32[]{:S(2)}) copy-start(f32[384,48]{0,1:T(8,128)} %param.37) | copy-start | bytes 221188
  936.0 11.9 %copy-start.49 = (f32[48,1536]{1,0:T(8,128)S(1)}, f32[48,1536]{1,0:T(8,128)}, u32[]{:S(2)}) copy-start(f32[48,1536]{1,0:T(8,128)} %param.26) | copy-start | bytes 884740
  936.0 11.9 %copy-start.69 = (f32[48,1536]{1,0:T(8,128)S(1)}, f32[48,1536]{1,0:T(8,128)}, u32[]{:S(2)}) copy-start(f32[48,1536]{1,0:T(8,128)} %param.32) | copy-start | bytes 884740
  936.0 11.9 %copy-start.70 = (f32[48,1536]{1,0:T(8,128)S(1)}, f32[48,1536]{1,0:T(8,128)}, u32[]{:S(2)}) copy-start(f32[48,1536]{1,0:T(8,128)} %param.38) | copy-start | bytes 884740
  948.0 4.8 copy-start.59
  948.0 4.8 copy-start.78
  948.0 4.8 copy-start.79
  (71 other events, 167.0 us)
Sparse Core Ops, SparseCore 0:
  11.3 62.8 all-gather.3
  96.2 18.0 all-reduce.11
  118.0 63.5 all-gather.5
  185.2 61.0 all-gather.7
  250.5 18.0 all-reduce.13
  290.5 20.4 all-reduce.15
  327.7 20.4 all-reduce.17
  360.4 20.4 all-reduce.19
  416.4 20.4 all-reduce.21
  452.8 20.4 all-reduce.23
  499.7 20.4 all-reduce.25
  526.5 399.5 all-reduce.27
where the time goes:
time: 970 us; the launch traced here: 962 us
  waiting for transfers between devices  552 us (57%)
  matrix products  134 us (14%)
  blocking collectives  132 us (14%)
  other arithmetic  76.9 us (8%)
  local copies, waits for them, and re-layouts  41.1 us (4%)
  between operations  24.7 us (3%)
    psum x1, waiting for transfers between devices, shards(): lax.psum((grad_qkv, grad_out, grad_up, grad_down, head_grad, shared_grad)...  314 us
    psum x1, blocking collectives, shards(): lax.psum((grad_qkv, grad_out, grad_up, grad_down, head_grad, shared_grad)...  81.7 us
    all_gather x1, waiting for transfers between devices, shards(): lax.all_gather(up_weight.astype(bfloat), 'dp', axis=0, tiled=True)  65.4 us
    all_gather x1, waiting for transfers between devices, shards(): lax.all_gather(down_weight.astype(bfloat), 'dp', axis=1, tiled=True)  53.2 us
    all_gather x1, blocking collectives, shards(): lax.all_gather(out_weight.astype(bfloat), 'dp', axis=1, tiled=True)  47 us
    psum x2, waiting for transfers between devices, shards(): lax.psum(attn_part.astype(jnp.bfloat16), 'head').astype(jnp.float32)  36.6 us
    psum x2, waiting for transfers between devices, shards(): lax.psum(ffn_part.astype(jnp.bfloat16), 'head').astype(jnp.float32)  31.5 us
    psum x2, waiting for transfers between devices, shards(): lax.psum(hidden_part.astype(jnp.bfloat16), 'head').astype(jnp.float32)  28.3 us
  transfers between devices with their start and end apart: 12, of which 12 were waited for; matrix products, arithmetic and copies ran while one was open for 8% of the time, Pallas kernels for 0%

commit v1 on v0

--- a/solution.py
+++ b/solution.py
@@ -114,7 +114,9 @@
             .astype(bfloat)
         )
         attn_part = jnp.einsum("cle,ed->cld", context_low, out_full, preferred_element_type=single)
-        attn_out = lax.psum(attn_part.astype(jnp.bfloat16), "head").astype(jnp.float32)
+        attn_out = jnp.sum(lax.all_gather(attn_part.astype(jnp.bfloat16), "head"), axis=0).astype(
+            jnp.float32
+        )
         first_in = layer_in + attn_out + out_bias
         hidden = norm_rows(first_in, gain_one, shift_one)
         hidden_low = hidden.astype(bfloat)

time: 970 us -> 956 us (0.986)
  waiting for transfers between devices: 552 us -> 526 us
    psum x2 -> x0, waiting for transfers between devices: 36.6 us -> none  [shards(): lax.psum(attn_part.astype(jnp.bfloat16), 'head').astype(jnp.float32)]
    all_gather x0 -> x2, waiting for transfers between devices: none -> 17.6 us  [shards(): lax.all_gather(attn_part.astype(jnp.bfloat16), 'head')]
    unnamed x246 -> x278, local copies, waits for them, and re-layouts: 19.2 us -> 21.9 us
  transfers between devices with their start and end apart: 12 -> 12, of which waited for: 12 -> 12; matrix products, arithmetic and copies ran while one was open for 8% -> 9% of each run, Pallas kernels for 0% -> 0%
where the time goes in v1:
time: 956 us; the launch traced here: 948 us
  waiting for transfers between devices  526 us (55%)
  matrix products  138 us (14%)
  blocking collectives  131 us (14%)
  other arithmetic  81.6 us (9%)
  local copies, waits for them, and re-layouts  44.4 us (5%)
  between operations  24.9 us (3%)
    psum x1, waiting for transfers between devices, shards(): lax.psum((grad_qkv, grad_out, grad_up, grad_down, head_grad, shared_grad)...  314 us
    psum x1, blocking collectives, shards(): lax.psum((grad_qkv, grad_out, grad_up, grad_down, head_grad, shared_grad)...  81.6 us
    all_gather x1, waiting for transfers between devices, shards(): lax.all_gather(up_weight.astype(bfloat), 'dp', axis=0, tiled=True)  61.2 us
    all_gather x1, waiting for transfers between devices, shards(): lax.all_gather(down_weight.astype(bfloat), 'dp', axis=1, tiled=True)  51.8 us
    all_gather x1, blocking collectives, shards(): lax.all_gather(out_weight.astype(bfloat), 'dp', axis=1, tiled=True)  46.8 us
    psum x2, waiting for transfers between devices, shards(): lax.psum(ffn_part.astype(jnp.bfloat16), 'head').astype(jnp.float32)  32.1 us
    psum x2, waiting for transfers between devices, shards(): lax.psum(hidden_part.astype(jnp.bfloat16), 'head').astype(jnp.float32)  27.7 us
    dot_general x2, matrix products, shards(): jnp.einsum('cld,de->cle', hidden_low, up_full, preferred_element_type=sin...  23.1 us
  transfers between devices with their start and end apart: 12, of which 12 were waited for; matrix products, arithmetic and copies ran while one was open for 9% of the time, Pallas kernels for 0%

profile of v1, /device:TPU:0, one launch (start us, length us, event | category | flops | bytes accessed | tf_op | source)
XLA Modules:
  0.0 948.5 jit_solution(16356854883026335976)
XLA Ops:
  12.1 46.8 %all_gather.25 = bf16[384,768]{0,1:T(8,128)(2,1)S(1)} all-gather(bf16[384,48]{0,1:T(8,128)(2,1)S(1)} %convert_element_type.455), channel_id=1, replica_groups=mesh['dp'=16,'head'=2] {'dp'}, dimensions={1}, use_global_device_ids=true | all-gather | bytes 626688 | tf_op jit(solution)/shard_map/all_gather | solution.py:78
  58.9 4.0 convert_bitcast_fusion.3
  62.9 12.1 %all-gather.10.cloned.1.call-done = bf16[3,768,384]{2,1,0:T(8,128)(2,1)} async-done(((bf16[3,48,384]{2,1,0:T(8,128)(2,1)}), bf16[3,768,384]{2,1,0:T(8,128)(2,1)}) %all-gather.10.cloned.1.call-update) | async-done | bytes 1769488 | tf_op jit(solution)/shard_map/all_gather | solution.py:77
  75.0 2.7 convolution_bitcast_fusion.1
  81.5 2.9 multiply_reduce_fusion.3
  89.2 5.3 convolution_convert_fusion.7
  99.2 6.6 all-gather.16.cloned.1.call-done
  105.8 2.2 reduce.66
  111.4 61.2 %all-gather.12.cloned.1.call-done = bf16[768,1536]{1,0:T(8,128)(2,1)} async-done(((bf16[48,1536]{1,0:T(8,128)(2,1)}), bf16[768,1536]{1,0:T(8,128)(2,1)}) %all-gather.12.cloned.1.call-update) | async-done | bytes 2359312 | tf_op jit(solution)/shard_map/all_gather | solution.py:79
  172.7 12.6 %multiply_convert_fusion.3 = (bf16[532,1536]{1,0:T(8,128)(2,1)}, f32[532,1536]{1,0:T(8,128)}, f32[532,1536]{1,0:T(8,128)}) fusion(f32[1536]{0:T(1024)S(1)} %slice_reduce_fusion, bf16[768,1536]{1,0:T(8,128)(2,1)} %all-gather.12.cloned.1.call-done, f32[768]{0:T(1024)S(1)} %get-tuple-element.101, f32[768]{0:T(1024)S(1)} %get-tuple-element.102, ...), kind=kOutput, calls=%fused_computation.37 | convolution fusion | flops 1313163264 | bytes 12971168 | tf_op jit(solution)/shard_map/cld,de->cle/dot_general | solution.py:124
  185.2 51.8 %all-gather.14.cloned.1.call-done = bf16[1536,768]{0,1:T(8,128)(2,1)} async-done(((bf16[1536,48]{0,1:T(8,128)(2,1)}), bf16[1536,768]{0,1:T(8,128)(2,1)}) %all-gather.14.cloned.1.call-update) | async-done | bytes 2359312 | tf_op jit(solution)/shard_map/all_gather | solution.py:80
  237.0 4.6 fusion.36
  243.7 16.1 %all-reduce.10.cloned.1.call-done = bf16[1,532,768]{2,1,0:T(8,128)(2,1)} async-done(((bf16[1,532,768]{2,1,0:T(8,128)(2,1)}), bf16[1,532,768]{2,1,0:T(8,128)(2,1)}) %all-reduce.10.cloned.1.call-update) | async-done | bytes 817168 | tf_op jit(solution)/shard_map/psum | solution.py:128
  274.6 5.0 convolution_convert_fusion.6
  282.3 11.0 %all-gather.18.cloned.1.call-done = bf16[2,532,768]{2,1,0:T(8,128)(2,1)} async-done(((bf16[1,532,768]{2,1,0:T(8,128)(2,1)}), bf16[2,532,768]{2,1,0:T(8,128)(2,1)}) %all-gather.18.cloned.1.call-update) | async-done | bytes 1634320 | tf_op jit(solution)/shard_map/all_gather | solution.py:117
  293.3 2.2 reduce.67
  295.5 2.2 fusion.67
  300.5 10.5 %multiply_convert_fusion.2 = (bf16[532,1536]{1,0:T(8,128)(2,1)S(1)}, f32[532,1536]{1,0:T(8,128)}, f32[532,1536]{1,0:T(8,128)}) fusion(f32[1536]{0:T(1024)S(1)} %copy-done.118, bf16[768,1536]{1,0:T(8,128)(2,1)S(1)} %copy-done.119, f32[532]{0:T(1024)S(1)} %fusion.89, f32[532]{0:T(1024)S(1)} %broadcast_multiply_fusion.2, f32[768]{0:T(1024)S(1)} %copy-done.105, ...), kind=kOutput, calls=%fused_computation.24 | convolution fusion | flops 1313163264 | bytes 12971168 | tf_op jit(solution)/shard_map/cld,de->cle/dot_general | solution.py:124
  312.3 2.4 fusion.37
  315.5 3.9 fusion.32
  319.4 15.9 %all-reduce.12.cloned.1.call-done = bf16[1,532,768]{2,1,0:T(8,128)(2,1)} async-done(((bf16[1,532,768]{2,1,0:T(8,128)(2,1)}), bf16[1,532,768]{2,1,0:T(8,128)(2,1)}) %all-reduce.12.cloned.1.call-update) | async-done | bytes 817168 | tf_op jit(solution)/shard_map/psum | solution.py:128
  335.3 2.4 fusion.132
  340.6 3.1 fusion.145
  344.9 2.4 fusion.38
  348.5 19.5 %all-reduce.14.cloned.1.call-done = bf16[1,532,768]{2,1,0:T(8,128)(2,1)} async-done(((bf16[1,532,768]{2,1,0:T(8,128)(2,1)}), bf16[1,532,768]{2,1,0:T(8,128)(2,1)}) %all-reduce.14.cloned.1.call-update) | async-done | bytes 817168 | tf_op jit(solution)/shard_map/psum | solution.py:200
  368.0 3.8 multiply_reduce_fusion.10
  375.2 2.0 copy.183
  377.2 6.0 fusion.143
  383.3 4.7 multiply_reduce_fusion.1
  388.0 2.1 multiply_convert_fusion.1
  390.2 2.2 fusion.44
  394.1 2.0 copy.189
  396.1 2.0 copy.188
  398.1 2.0 copy.187
  400.0 4.1 fusion.42
  404.4 6.4 fusion.113
  410.8 4.6 fusion.56
  415.4 2.0 fusion.110
  417.4 7.3 all-reduce.16.cloned.1.call-done
  424.7 2.1 add_reduce_fusion.2
  428.7 2.4 multiply_reduce_fusion.7
  433.1 2.7 fusion.146
  437.0 2.4 fusion.39
  439.7 4.9 fusion.69
  444.6 7.3 convolution_add_fusion.1
  451.8 8.2 all-reduce.18.cloned.1.call-done
  460.0 2.1 multiply_reduce_fusion.8
  465.2 5.1 fusion.142
  470.3 5.0 multiply_reduce_fusion
  475.3 2.1 multiply_convert_fusion
  482.1 3.9 fusion.43
  486.1 7.3 convolution_add_fusion
  495.4 3.7 add_bitcast_fusion
  500.6 3.7 fusion.60
  504.5 2.1 all-reduce.20.cloned.1.call-done
  506.7 2.7 add_reduce_fusion
  510.3 81.6 %all-reduce = (f32[1,2304]{1,0:T(1,128)S(1)}, f32[16,768]{1,0:T(8,128)S(1)}) all-reduce(f32[1,2304]{1,0:T(1,128)S(1)} %broadcast_in_dim.92, f32[16,768]{1,0:T(8,128)S(1)} %pad_maximum_fusion.12), channel_id=1, replica_groups=mesh['dp'=16,'head'=2] {'dp'}, use_global_device_ids=true, to_apply=%region_44.45 | all-reduce | flops 14592 | bytes 116736 | tf_op jit(solution)/shard_map/psum | solution.py:264
  592.5 3.0 fusion.59
  598.4 314.2 %all-reduce.22.cloned.1.call-done = (f32[3,768,384]{2,1,0:T(8,128)}, f32[384,768]{0,1:T(8,128)}, f32[768,1536]{1,0:T(8,128)}, f32[1536,768]{0,1:T(8,128)}) async-done(((f32[3,768,384]{2,1,0:T(8,128)}, f32[384,768]{0,1:T(8,128)}, f32[768,1536]{1,0:T(8,128)}, f32[1536,768]{0,1:T(8,128)}), (f32[3,768,384]{2,1,0:T(8,128)}, f32[384,768]{0,1:T(8,128)}, f32[768,1536]{1,0:T(8,128)}, ...) | async-done | bytes 14155792 | tf_op jit(solution)/shard_map/psum | solution.py:264
  912.5 3.7 multiply_reduce_fusion.6
  916.2 2.2 multiply_reduce_fusion.19
  926.5 3.0 psum.102
  934.5 2.1 multiply_subtract_fusion.1
  936.6 2.0 multiply_subtract_fusion
  (413 shorter events, 84.0 us)
Async XLA Ops:
  7.2 67.8 %all-gather.10.cloned.1.call-start = ((), (), s32[]{:S(2)}) async-start(), calls=%async_computation | async-start | bytes 1880064 | tf_op jit(solution)/shard_map/all_gather | solution.py:77
  8.9 96.9 %all-gather.16.cloned.1.call-start = ((), (), s32[]{:S(2)}) async-start(), calls=%async_computation.9 | async-start | bytes 2469888 | tf_op jit(solution)/shard_map/all_gather | solution.py:117
  9.8 79.4 %copy-start.86 = (f32[6,64]{1,0:T(8,128)}, f32[6,64]{1,0:T(8,128)S(1)}, u32[]{:S(2)}) copy-start(f32[6,64]{1,0:T(8,128)S(1)} %add.565) | copy-start | bytes 4612
  58.9 35.6 %copy-start.40 = (bf16[384,768]{0,1:T(8,128)(2,1)}, bf16[384,768]{0,1:T(8,128)(2,1)S(1)}, u32[]{:S(2)}) copy-start(bf16[384,768]{0,1:T(8,128)(2,1)S(1)} %all_gather.25) | copy-start | bytes 1769476
  62.9 109.8 %copy-start.14 = (f32[512,768]{1,0:T(8,128)}, f32[512,768]{1,0:T(8,128)S(1)}, u32[]{:S(2)}) copy-start(f32[512,768]{1,0:T(8,128)S(1)} %get-tuple-element.165) | copy-start | bytes 4718596
  89.2 5.3 copy-start.21
  96.9 75.7 %all-gather.12.cloned.1.call-start = ((), (), s32[]{:S(2)}) async-start(), calls=%async_computation.1 | async-start | bytes 2506752 | tf_op jit(solution)/shard_map/all_gather | solution.py:79
  97.7 139.3 %all-gather.14.cloned.1.call-start = ((), (), s32[]{:S(2)}) async-start(), calls=%async_computation.2 | async-start | bytes 2506752 | tf_op jit(solution)/shard_map/all_gather | solution.py:80
  98.5 161.4 %all-reduce.10.cloned.1.call-start = ((), (), s32[]{:S(2)}) async-start(), calls=%async_computation.3 | async-start | bytes 1646592 | tf_op jit(solution)/shard_map/psum | solution.py:128
  99.1 73.6 %copy-start.117 = (f32[1536]{0:T(1024)}, f32[1536]{0:T(1024)S(1)}, u32[]{:S(2)}) copy-start(f32[1536]{0:T(1024)S(1)} %slice_reduce_fusion) | copy-start | bytes 18436
  99.2 73.5 %copy-start.84 = (f32[768]{0:T(1024)}, f32[768]{0:T(1024)S(1)}, u32[]{:S(2)}) copy-start(f32[768]{0:T(1024)S(1)} %get-tuple-element.103) | copy-start | bytes 9220
  99.2 160.7 %copy-start.104 = (f32[768]{0:T(1024)}, f32[768]{0:T(1024)S(1)}, u32[]{:S(2)}) copy-start(f32[768]{0:T(1024)S(1)} %get-tuple-element.101) | copy-start | bytes 9220
  99.2 160.7 %copy-start.106 = (f32[768]{0:T(1024)}, f32[768]{0:T(1024)S(1)}, u32[]{:S(2)}) copy-start(f32[768]{0:T(1024)S(1)} %get-tuple-element.100) | copy-start | bytes 9220
  99.2 162.8 %copy-start.96 = (f32[768]{0:T(1024)}, f32[768]{0:T(1024)S(1)}, u32[]{:S(2)}) copy-start(f32[768]{0:T(1024)S(1)} %get-tuple-element.104) | copy-start | bytes 9220
  108.4 64.3 %copy-start.109 = (f32[532]{0:T(1024)}, f32[532]{0:T(1024)S(1)}, u32[]{:S(2)}) copy-start(f32[532]{0:T(1024)S(1)} %broadcast_multiply_fusion.4) | copy-start | bytes 6388
  111.4 73.9 %copy-start.102 = (f32[532]{0:T(1024)}, f32[532]{0:T(1024)S(1)}, u32[]{:S(2)}) copy-start(f32[532]{0:T(1024)S(1)} %get-tuple-element.152) | copy-start | bytes 6388
  111.4 148.5 %copy-start.2 = (f32[1,532,768]{2,1,0:T(8,128)}, f32[1,532,768]{2,1,0:T(8,128)S(1)}, u32[]{:S(2)}) copy-start(f32[1,532,768]{2,1,0:T(8,128)S(1)} %get-tuple-element.153) | copy-start | bytes 4902916
  111.4 148.5 %copy-start.92 = (f32[532]{0:T(1024)}, f32[532]{0:T(1024)S(1)}, u32[]{:S(2)}) copy-start(f32[532]{0:T(1024)S(1)} %fusion.87) | copy-start | bytes 6388
  241.6 51.7 %all-gather.18.cloned.1.call-start = ((), (), s32[]{:S(2)}) async-start(), calls=%async_computation.10 | async-start | bytes 2469888 | tf_op jit(solution)/shard_map/all_gather | solution.py:117
  274.3 5.4 copy-start.23
  274.6 5.8 copy-start.41
  282.0 13.5 %copy-start.75 = (f32[1,10,768]{2,1,0:T(8,128)S(1)}, f32[1,10,768]{2,1,0:T(8,128)}, u32[]{:S(2)}) copy-start(f32[1,10,768]{2,1,0:T(8,128)} %copy-done.74) | copy-start | bytes 92164
  282.0 13.5 %copy-start.85 = (f32[768]{0:T(1024)S(1)}, f32[768]{0:T(1024)}, u32[]{:S(2)}) copy-start(f32[768]{0:T(1024)} %copy-done.84) | copy-start | bytes 9220
  282.1 53.3 %all-reduce.12.cloned.1.call-start = ((), (), s32[]{:S(2)}) async-start(), calls=%async_computation.4 | async-start | bytes 1646592 | tf_op jit(solution)/shard_map/psum | solution.py:128
  300.5 11.8 %copy-start.122 = (bf16[1536,768]{0,1:T(8,128)(2,1)S(1)}, bf16[1536,768]{0,1:T(8,128)(2,1)}, u32[]{:S(2)}) copy-start(bf16[1536,768]{0,1:T(8,128)(2,1)} %all-gather.14.cloned.1.call-done) | copy-start | bytes 7077892
  314.7 53.3 %all-reduce.14.cloned.1.call-start = ((), (), s32[]{:S(2)}) async-start(), calls=%async_computation.5 | async-start | bytes 1646592 | tf_op jit(solution)/shard_map/psum | solution.py:200
  315.5 19.8 %copy-start.107 = (f32[768]{0:T(1024)S(1)}, f32[768]{0:T(1024)}, u32[]{:S(2)}) copy-start(f32[768]{0:T(1024)} %copy-done.106) | copy-start | bytes 9220
  347.4 77.4 %all-reduce.16.cloned.1.call-start = ((), (), s32[]{:S(2)}) async-start(), calls=%async_computation.6 | async-start | bytes 1646592 | tf_op jit(solution)/shard_map/psum | solution.py:244
  377.2 6.0 copy-start.24
  377.2 6.0 copy-start.50
  377.2 10.8 %slice-start.2 = ((s8[8232960]{0:T(1024)(128)(4,1)}), s8[4194304]{0:T(1024)(128)(4,1)S(1)}, s32[]{:S(2)}) async-start(s8[8232960]{0:T(1024)(128)(4,1)} %bitcast.211), calls=%async_computation.14 | async-start | bytes 8388608
  404.1 6.7 copy-start.113
  404.1 55.9 %all-reduce.18.cloned.1.call-start = ((), (), s32[]{:S(2)}) async-start(), calls=%async_computation.7 | async-start | bytes 1646592 | tf_op jit(solution)/shard_map/psum | solution.py:200
  404.3 6.4 copy-start.28
  404.4 6.4 copy-start.34
  404.4 6.4 copy-start.130
  417.4 11.2 %copy-start.91 = (f32[532]{0:T(1024)S(1)}, f32[532]{0:T(1024)}, u32[]{:S(2)}) copy-start(f32[532]{0:T(1024)} %copy-done.90) | copy-start | bytes 6388
  439.3 5.2 copy-start.93
  439.4 5.2 copy-start.110
  439.4 67.3 %all-reduce.20.cloned.1.call-start = ((), (), s32[]{:S(2)}) async-start(), calls=%async_computation.8 | async-start | bytes 1646592 | tf_op jit(solution)/shard_map/psum | solution.py:244
  439.6 4.9 copy-start.15
  439.6 4.9 copy-start.26
  439.7 4.9 copy-start.128
  444.6 15.4 %copy-start.3 = (f32[1,532,768]{2,1,0:T(8,128)S(1)}, f32[1,532,768]{2,1,0:T(8,128)}, u32[]{:S(2)}) copy-start(f32[1,532,768]{2,1,0:T(8,128)} %copy-done.2) | copy-start | bytes 4902916
  451.8 10.3 %copy-start.103 = (f32[532]{0:T(1024)S(1)}, f32[532]{0:T(1024)}, u32[]{:S(2)}) copy-start(f32[532]{0:T(1024)} %copy-done.102) | copy-start | bytes 6388
  465.2 5.2 copy-start.22
  465.2 10.1 %slice-start = ((s8[8232960]{0:T(1024)(128)(4,1)}), s8[4194304]{0:T(1024)(128)(4,1)S(1)}, s32[]{:S(2)}) async-start(s8[8232960]{0:T(1024)(128)(4,1)} %bitcast.209), calls=%async_computation.12 | async-start | bytes 8388608
  470.3 5.0 slice-start.1
  486.0 7.4 copy-start.8
  486.0 426.5 %all-reduce.22.cloned.1.call-start = ((), (), s32[]{:S(2)}) async-start(), calls=%async_computation.11 | async-start | bytes 28311552 | tf_op jit(solution)/shard_map/psum | solution.py:264
  486.1 7.4 copy-start.44
  486.1 7.4 copy-start.52
  486.1 9.3 copy-start.53
  912.5 5.8 copy-start.39
  920.7 10.1 %copy-start.69 = (f32[3,48,384]{2,1,0:T(8,128)S(1)}, f32[3,48,384]{2,1,0:T(8,128)}, u32[]{:S(2)}) copy-start(f32[3,48,384]{2,1,0:T(8,128)} %param.24) | copy-start | bytes 663556
  920.7 10.1 %copy-start.81 = (f32[3,48,384]{2,1,0:T(8,128)S(1)}, f32[3,48,384]{2,1,0:T(8,128)}, u32[]{:S(2)}) copy-start(f32[3,48,384]{2,1,0:T(8,128)} %param.30) | copy-start | bytes 663556
  920.7 10.1 %copy-start.82 = (f32[3,48,384]{2,1,0:T(8,128)S(1)}, f32[3,48,384]{2,1,0:T(8,128)}, u32[]{:S(2)}) copy-start(f32[3,48,384]{2,1,0:T(8,128)} %param.36) | copy-start | bytes 663556
  922.5 10.2 %copy-start.80 = (f32[384,48]{0,1:T(8,128)S(1)}, f32[384,48]{0,1:T(8,128)}, u32[]{:S(2)}) copy-start(f32[384,48]{0,1:T(8,128)} %param.25) | copy-start | bytes 221188
  922.5 10.2 %copy-start.88 = (f32[384,48]{0,1:T(8,128)S(1)}, f32[384,48]{0,1:T(8,128)}, u32[]{:S(2)}) copy-start(f32[384,48]{0,1:T(8,128)} %param.31) | copy-start | bytes 221188
  922.5 10.2 %copy-start.89 = (f32[384,48]{0,1:T(8,128)S(1)}, f32[384,48]{0,1:T(8,128)}, u32[]{:S(2)}) copy-start(f32[384,48]{0,1:T(8,128)} %param.37) | copy-start | bytes 221188
  922.5 11.9 %copy-start.66 = (f32[48,1536]{1,0:T(8,128)S(1)}, f32[48,1536]{1,0:T(8,128)}, u32[]{:S(2)}) copy-start(f32[48,1536]{1,0:T(8,128)} %param.26) | copy-start | bytes 884740
  922.5 11.9 %copy-start.76 = (f32[48,1536]{1,0:T(8,128)S(1)}, f32[48,1536]{1,0:T(8,128)}, u32[]{:S(2)}) copy-start(f32[48,1536]{1,0:T(8,128)} %param.32) | copy-start | bytes 884740
  922.5 11.9 %copy-start.77 = (f32[48,1536]{1,0:T(8,128)S(1)}, f32[48,1536]{1,0:T(8,128)}, u32[]{:S(2)}) copy-start(f32[48,1536]{1,0:T(8,128)} %param.38) | copy-start | bytes 884740
  934.5 4.8 copy-start.71
  (87 other events, 215.7 us)
Sparse Core Ops, SparseCore 0:
  11.3 63.6 all-gather.9
  97.1 8.6 all-gather.15
  109.1 63.4 all-gather.11
  175.9 61.0 all-gather.13
  241.7 18.0 all-reduce.9
  282.2 11.1 all-gather.17
  314.8 20.4 all-reduce.11
  347.5 20.4 all-reduce.13
  404.2 20.4 all-reduce.15
  439.5 20.4 all-reduce.17
  486.1 20.4 all-reduce.19
  513.0 399.5 all-reduce.21
